TPU v7x, 256 devices: a whole 4x4x8 slice. The times are simulated.
256 devices in a mesh: dp: 32 (over y, z_hi, core), factor: 8 (over z_lo, x).
Axes of the slice: x: 4, y: 4, z: 8 (z_hi: 4, z_lo: 2; z = z_hi * 2 + z_lo), core: 2. Of those that a mesh axis runs over, the one named last changes fastest.
Arguments:
- grad_out: bfloat16 [32, 128, 14336], P('dp', None, 'factor'), may hold values from -6 to 6
- act_in: bfloat16 [32, 128, 4096], P('dp', None, 'factor'), may hold values from -6 to 6
- basis_out: bfloat16 [14336, 14336], P('factor', 'dp'), may hold values from -0.046875 to 0.046875
- basis_in: bfloat16 [4096, 4096], P('factor', 'dp'), may hold values from -0.09375 to 0.09375
- eigen_vals: bfloat16 [14336, 4096], P('dp'), may hold values from 0.25 to 4
- query_out: bfloat16 [16, 8, 14336], P(None, None, 'factor'), may hold values from -0.01171875 to 0.01171875
- query_in: bfloat16 [16, 8, 4096], P(None, None, 'factor'), may hold values from -0.01171875 to 0.01171875
Outputs:
- scores: float32 [32, 16], P('factor')
All inputs are finite; a program needn't handle non-finite values.
Results may differ from a plain program's by a relative error of at most 0.023.
Values may be sent and summed in bfloat16 or wider, within the bound.
No kernel may reach another device: no remote copies, remote signals or barrier semaphores. Data moves between devices by JAX's collectives and lax.ppermute only.
A program may use at most 128 MiB of HBM per device.

v0:
```python
import jax
import jax.numpy as jnp
from jax import lax
from jax.sharding import PartitionSpec as P


def shards(grad_out, act_in, basis_out, basis_in, eigen_vals, query_out, query_in):
    shard_part = lax.all_gather(grad_out, "dp", axis=0, tiled=True)
    flattened = shard_part.reshape(-1, shard_part.shape[2])
    product = jnp.dot(flattened, basis_out, preferred_element_type=jnp.float32)
    partial_value = product.reshape(shard_part.shape[0], shard_part.shape[1], -1)
    grad_sum = lax.psum_scatter(
        partial_value.astype(jnp.bfloat16), "factor", scatter_dimension=0, tiled=True
    )
    shard_part = lax.all_gather(act_in, "dp", axis=0, tiled=True)
    flattened = shard_part.reshape(-1, shard_part.shape[2])
    product = jnp.dot(flattened, basis_in, preferred_element_type=jnp.float32)
    act_part = product.reshape(shard_part.shape[0], shard_part.shape[1], -1)
    act_sum = lax.psum_scatter(
        act_part.astype(jnp.bfloat16), "factor", scatter_dimension=0, tiled=True
    )
    act_rot = lax.all_gather(act_sum, "dp", axis=2, tiled=True)
    query_part = jnp.einsum("qrk,ki->qri", query_out, basis_out, preferred_element_type=jnp.float32)
    value_part = jnp.einsum("qrk,kj->qrj", query_in, basis_in, preferred_element_type=jnp.float32)
    query_rot, value_sum = (
        lax.psum(query_part.astype(jnp.bfloat16), "factor").astype(jnp.float32),
        lax.psum(value_part.astype(jnp.bfloat16), "factor").astype(jnp.float32),
    )
    value_rot = lax.all_gather(value_sum.astype(jnp.bfloat16), "dp", axis=2, tiled=True)
    query_count = value_rot.shape[0]
    rank_count = value_rot.shape[1]
    value_mat = value_rot.reshape(query_count * rank_count, value_rot.shape[2])
    eigen_float = eigen_vals.astype(jnp.float32)

    def per_sequence(operands):
        contracted = lax.dot_general(
            operands[0], operands[1], (((0,), (0,)), ((), ())), preferred_element_type=jnp.float32
        )
        scaled = (contracted / eigen_float).astype(jnp.bfloat16)
        weighted = lax.dot_general(
            scaled, value_mat, (((1,), (1,)), ((), ())), preferred_element_type=jnp.float32
        )
        weighted = weighted.reshape(weighted.shape[0], query_count, rank_count)
        return jnp.einsum("iqr,qri->q", weighted, query_rot)

    partial_scores = lax.map(per_sequence, (grad_sum, act_rot))
    return lax.psum(partial_scores, "dp")


def solution(mesh):
    in_specs = (
        P("dp", None, "factor"),
        P("dp", None, "factor"),
        P("factor", "dp"),
        P("factor", "dp"),
        P("dp", None),
        P(None, None, "factor"),
        P(None, None, "factor"),
    )
    out_specs = P("factor", None)
    return jax.shard_map(shards, mesh=mesh, in_specs=in_specs, out_specs=out_specs, check_vma=False)
```

profile of v0, /device:TPU:2, one launch (start us, length us, event | category | flops | bytes accessed | tf_op | source)
XLA Modules:
  0.0 580.7 jit_solution(15563203050592164116)
XLA Ops:
  6.5 0.0 copy-start
  6.5 0.0 copy-start.2
  6.5 0.0 all-gather.7.cloned.1.call-start
  6.5 0.7 all-gather.7.cloned.1.call-update
  7.3 0.0 copy-start.1
  7.3 0.0 copy-start.3
  7.3 0.0 reduce-scatter.5.cloned.1.call-start
  7.3 65.9 %all-gather.7.cloned.1.call-done = bf16[32,128,512]{2,1,0:T(8,128)(2,1)} async-done(((bf16[1,128,512]{2,1,0:T(8,128)(2,1)}), bf16[32,128,512]{2,1,0:T(8,128)(2,1)}) %all-gather.7.cloned.1.call-update) | async-done | bytes 4194320 | tf_op jit(solution)/shard_map/all_gather | solution.py:15
  73.2 4.4 convolution_convert_fusion.1
  77.6 0.0 reduce-scatter.5.cloned.1.call-update
  77.7 0.0 all-gather.5.cloned.1.call-start
  77.7 0.7 all-gather.5.cloned.1.call-update
  78.4 0.0 all-reduce.2.cloned.1.call-start
  78.5 0.0 copy-done
  78.5 0.0 copy-done.2
  78.5 1.3 fusion.17
  79.7 0.0 all-reduce.2.cloned.1.call-update
  79.8 0.0 all-gather.11.cloned.1.call-start
  79.8 0.0 copy-done.1
  79.8 0.0 copy-done.3
  79.8 0.2 convolution_convert_fusion.2
  80.0 30.1 %psum.21 = bf16[16,8,128]{2,1,0:T(8,128)(2,1)} all-reduce(bf16[16,8,128]{2,1,0:T(8,128)(2,1)S(1)} %convolution_convert_fusion.2), channel_id=1, replica_groups=mesh['dp'=32,'factor'=8] {'factor'}, use_global_device_ids=true, to_apply=%region_2.0 | all-reduce | flops 16384 | bytes 65536 | tf_op jit(solution)/shard_map/psum | solution.py:27
  110.1 0.0 all-gather.11.cloned.1.call-update
  110.1 0.0 all-gather.9.cloned.1.call-start
  110.2 5.2 reduce-scatter.5.cloned.1.call-done
  115.4 0.0 all-gather.9.cloned.1.call-update
  115.4 0.0 reduce-scatter.3.cloned.1.call-start
  115.4 101.9 %all-gather.5.cloned.1.call-done = bf16[32,128,1792]{2,1,0:T(8,128)(2,1)} async-done(((bf16[1,128,1792]{2,1,0:T(8,128)(2,1)}), bf16[32,128,1792]{2,1,0:T(8,128)(2,1)}) %all-gather.5.cloned.1.call-update) | async-done | bytes 14680080 | tf_op jit(solution)/shard_map/all_gather | solution.py:8
  217.4 11.6 %convolution_convert_fusion = bf16[32,128,448]{1,2,0:T(8,128)(2,1)} fusion(bf16[32,128,1792]{2,1,0:T(8,128)(2,1)} %all-gather.5.cloned.1.call-done, bf16[1792,448]{0,1:T(8,128)(2,1)S(1)} %copy-done), kind=kOutput, calls=%fused_computation.10 | convolution fusion | flops 6578503680 | bytes 19955712 | tf_op jit(solution)/shard_map/dot_general | solution.py:10
  229.0 0.0 reduce-scatter.3.cloned.1.call-update
  229.0 5.9 %convert_element_type.25 = f32[448,4096]{1,0:T(8,128)} convert(bf16[448,4096]{1,0:T(8,128)(2,1)} %param.13) | non-fusion elementwise | flops 1835008 | bytes 11010048 | tf_op jit(solution)/shard_map/convert_element_type | solution.py:33
  234.9 71.2 %all-reduce.2.cloned.1.call-done = bf16[16,8,448]{2,1,0:T(8,128)(2,1)} async-done(((bf16[16,8,448]{2,1,0:T(8,128)(2,1)}), bf16[16,8,448]{2,1,0:T(8,128)(2,1)}) %all-reduce.2.cloned.1.call-update) | async-done | bytes 114704 | tf_op jit(solution)/shard_map/psum | solution.py:26
  306.1 0.9 convert_element_type.28
  307.0 55.1 %all-gather.11.cloned.1.call-done = bf16[16,8,4096]{2,1,0:T(8,128)(2,1)} async-done(((bf16[16,8,128]{2,1,0:T(8,128)(2,1)}), bf16[16,8,4096]{2,1,0:T(8,128)(2,1)}) %all-gather.11.cloned.1.call-update) | async-done | bytes 1048592 | tf_op jit(solution)/shard_map/all_gather | solution.py:29
  362.1 63.3 %all-gather.9.cloned.1.call-done = bf16[4,128,4096]{2,1,0:T(8,128)(2,1)} async-done(((bf16[4,128,128]{2,1,0:T(8,128)(2,1)}), bf16[4,128,4096]{2,1,0:T(8,128)(2,1)}) %all-gather.9.cloned.1.call-update) | async-done | bytes 4194320 | tf_op jit(solution)/shard_map/all_gather | solution.py:22
  425.5 50.1 %reduce-scatter.3.cloned.1.call-done = bf16[4,128,448]{1,2,0:T(8,128)(2,1)} async-done(((bf16[32,128,448]{1,2,0:T(8,128)(2,1)}), bf16[4,128,448]{1,2,0:T(8,128)(2,1)}) %reduce-scatter.3.cloned.1.call-update) | async-done | bytes 458768 | tf_op jit(solution)/shard_map/reduce_scatter | solution.py:12
  475.6 24.1 %while.10 = (s32[]{:T(128)}, f32[4,16]{1,0:T(4,128)S(1)}, bf16[4,128,448]{1,2,0:T(8,128)(2,1)}, bf16[4,128,4096]{2,1,0:T(8,128)(2,1)}, f32[448,4096]{1,0:T(8,128...) while((s32[]{:T(128)}, f32[4,16]{1,0:T(4,128)S(1)}, ...), condition=%wide.region_5.6_spmd, body=%wide.region_4.5_spmd.sunk | while | flops 943308800 | bytes 9782569 | solution.py:46
  475.6 6.0 %fusion.34 = f32[16]{0:T(128)S(1)} fusion(bf16[128,4096]{1,0:T(8,128)(2,1)} %get-tuple-element.144, f32[448,4096]{1,0:T(8,128)} %get-tuple-element.143, bf16[4,128,4096]{2,1,0:T(8,128)(2,1)} %get-tuple-element.142, s32[]{:T(128)S(6)} %copy.25, f32[16,8,448]{2,1,0:T(8,128)S(1)} %get-tuple-element.145, bf16[4,128,448]{1,2,0:T(8,128)(2,1)} %get-tuple-element.141), kind=kOutput, calls=%fused_computation.4.clone.1 | convolution fusion | flops 943308800 | bytes 9782336 | tf_op jit(solution)/shard_map/while/body/eval_jaxpr/dot_general | solution.py:40
  481.6 6.0 %fusion.34 = f32[16]{0:T(128)S(1)} fusion(bf16[128,4096]{1,0:T(8,128)(2,1)} %get-tuple-element.144, f32[448,4096]{1,0:T(8,128)} %get-tuple-element.143, bf16[4,128,4096]{2,1,0:T(8,128)(2,1)} %get-tuple-element.142, s32[]{:T(128)S(6)} %copy.25, f32[16,8,448]{2,1,0:T(8,128)S(1)} %get-tuple-element.145, bf16[4,128,448]{1,2,0:T(8,128)(2,1)} %get-tuple-element.141), kind=kOutput, calls=%fused_computation.4.clone.1 | convolution fusion | flops 943308800 | bytes 9782336 | tf_op jit(solution)/shard_map/while/body/eval_jaxpr/dot_general | solution.py:40
  487.6 6.0 %fusion.34 = f32[16]{0:T(128)S(1)} fusion(bf16[128,4096]{1,0:T(8,128)(2,1)} %get-tuple-element.144, f32[448,4096]{1,0:T(8,128)} %get-tuple-element.143, bf16[4,128,4096]{2,1,0:T(8,128)(2,1)} %get-tuple-element.142, s32[]{:T(128)S(6)} %copy.25, f32[16,8,448]{2,1,0:T(8,128)S(1)} %get-tuple-element.145, bf16[4,128,448]{1,2,0:T(8,128)(2,1)} %get-tuple-element.141), kind=kOutput, calls=%fused_computation.4.clone.1 | convolution fusion | flops 943308800 | bytes 9782336 | tf_op jit(solution)/shard_map/while/body/eval_jaxpr/dot_general | solution.py:40
  493.6 6.0 %fusion.34 = f32[16]{0:T(128)S(1)} fusion(bf16[128,4096]{1,0:T(8,128)(2,1)} %get-tuple-element.144, f32[448,4096]{1,0:T(8,128)} %get-tuple-element.143, bf16[4,128,4096]{2,1,0:T(8,128)(2,1)} %get-tuple-element.142, s32[]{:T(128)S(6)} %copy.25, f32[16,8,448]{2,1,0:T(8,128)S(1)} %get-tuple-element.145, bf16[4,128,448]{1,2,0:T(8,128)(2,1)} %get-tuple-element.141), kind=kOutput, calls=%fused_computation.4.clone.1 | convolution fusion | flops 943308800 | bytes 9782336 | tf_op jit(solution)/shard_map/while/body/eval_jaxpr/dot_general | solution.py:40
  499.7 74.2 %psum.23 = f32[4,16]{1,0:T(4,128)} all-reduce(f32[4,16]{1,0:T(4,128)S(1)} %get-tuple-element.42), channel_id=1, replica_groups=mesh['dp'=32,'factor'=8] {'dp'}, use_global_device_ids=true, to_apply=%region_6.7 | all-reduce | flops 64 | bytes 512 | tf_op jit(solution)/shard_map/psum | solution.py:47
  (5 shorter events, 0.1 us)
Async XLA Ops:
  6.5 71.9 %copy-start = (bf16[1792,448]{0,1:T(8,128)(2,1)S(1)}, bf16[1792,448]{0,1:T(8,128)(2,1)}, u32[]{:S(2)}) copy-start(bf16[1792,448]{0,1:T(8,128)(2,1)} %param.11) | copy-start | bytes 4816900
  6.5 71.9 %copy-start.2 = (bf16[16,8,1792]{2,1,0:T(8,128)(2,1)S(1)}, bf16[16,8,1792]{2,1,0:T(8,128)(2,1)}, u32[]{:S(2)}) copy-start(bf16[16,8,1792]{2,1,0:T(8,128)(2,1)} %param.14) | copy-start | bytes 1376260
  6.5 66.7 %all-gather.7.cloned.1.call-start = ((), (), s32[]{:S(2)}) async-start(), calls=%async_computation.4 | async-start | bytes 4325376 | tf_op jit(solution)/shard_map/all_gather | solution.py:15
  7.3 72.6 %copy-start.1 = (bf16[512,128]{1,0:T(8,128)(2,1)S(1)}, bf16[512,128]{1,0:T(8,128)(2,1)}, u32[]{:S(2)}) copy-start(bf16[512,128]{1,0:T(8,128)(2,1)} %param.12) | copy-start | bytes 393220
  7.3 72.6 %copy-start.3 = (bf16[16,8,512]{2,1,0:T(8,128)(2,1)S(1)}, bf16[16,8,512]{2,1,0:T(8,128)(2,1)}, u32[]{:S(2)}) copy-start(bf16[16,8,512]{2,1,0:T(8,128)(2,1)} %param.15) | copy-start | bytes 393220
  7.3 108.1 %reduce-scatter.5.cloned.1.call-start = ((), (), s32[]{:S(2)}) async-start(), calls=%async_computation.5 | async-start | bytes 1179648 | tf_op jit(solution)/shard_map/reduce_scatter | solution.py:19
  77.7 139.7 %all-gather.5.cloned.1.call-start = ((), (), s32[]{:S(2)}) async-start(), calls=%async_computation.2 | async-start | bytes 15138816 | tf_op jit(solution)/shard_map/all_gather | solution.py:8
  78.4 227.7 %all-reduce.2.cloned.1.call-start = ((), (), s32[]{:S(2)}) async-start(), calls=%async_computation.8 | async-start | bytes 262144 | tf_op jit(solution)/shard_map/psum | solution.py:26
  79.8 282.4 %all-gather.11.cloned.1.call-start = ((), (), s32[]{:S(2)}) async-start(), calls=%async_computation.7 | async-start | bytes 1081344 | tf_op jit(solution)/shard_map/all_gather | solution.py:29
  110.1 315.4 %all-gather.9.cloned.1.call-start = ((), (), s32[]{:S(2)}) async-start(), calls=%async_computation.6 | async-start | bytes 4325376 | tf_op jit(solution)/shard_map/all_gather | solution.py:22
  115.4 360.2 %reduce-scatter.3.cloned.1.call-start = ((), (), s32[]{:S(2)}) async-start(), calls=%async_computation.3 | async-start | bytes 4128768 | tf_op jit(solution)/shard_map/reduce_scatter | solution.py:12
Sparse Core Ops, SparseCore 0:
  9.9 63.2 all-gather.6
  77.8 37.5 reduce-scatter.4
  117.9 99.4 all-gather.4
  219.8 86.1 all-reduce.1
  308.4 53.7 all-gather.10
  364.5 60.9 all-gather.8
  428.0 47.4 reduce-scatter.2
where the time goes:
time: 581 us
  waiting for transfers between devices  414 us (71%)
  blocking collectives  104 us (18%)
  matrix products  41.4 us (7%)
  between operations  13.6 us (2%)
  other arithmetic  6.81 us (1%)
    all_gather x1, waiting for transfers between devices, shards(): shard_part = lax.all_gather(grad_out, 'dp', axis=0, tiled=True)  102 us
    psum x1, blocking collectives, shards(): return lax.psum(partial_scores, 'dp')  74.2 us
    psum x1, waiting for transfers between devices, shards(): lax.psum(query_part.astype(jnp.bfloat16), 'factor').astype(jnp.float32)  71.2 us
    all_gather x1, waiting for transfers between devices, shards(): shard_part = lax.all_gather(act_in, 'dp', axis=0, tiled=True)  65.9 us
    all_gather x1, waiting for transfers between devices, shards(): act_rot = lax.all_gather(act_sum, 'dp', axis=2, tiled=True)  63.3 us
    all_gather x1, waiting for transfers between devices, shards(): lax.all_gather(value_sum.astype(jnp.bfloat16), 'dp', axis=2, tiled=True)  55.1 us
    reduce_scatter x1, waiting for transfers between devices, shards(): lax.psum_scatter(partial_value.astype(jnp.bfloat16), 'factor', scatter_di...  50.1 us
    psum x1, blocking collectives, shards(): lax.psum(value_part.astype(jnp.bfloat16), 'factor').astype(jnp.float32)  30.1 us
  transfers between devices with their start and end apart: 7, of which 7 were waited for; matrix products, arithmetic and copies ran while one was open for 3% of the time, Pallas kernels for 0%

commit v1 on v0

--- a/solution.py
+++ b/solution.py
@@ -2,6 +2,11 @@
 import jax.numpy as jnp
 from jax import lax
 from jax.sharding import PartitionSpec as P
+
+
+def swapped_in(x, axis, d):
+    outgoing = jnp.stack([x] * lax.axis_size(axis))
+    return jnp.concatenate(lax.all_to_all(outgoing, axis, 0, 0), axis=d)
 
 
 def shards(grad_out, act_in, basis_out, basis_in, eigen_vals, query_out, query_in):
@@ -12,7 +17,7 @@
     grad_sum = lax.psum_scatter(
         partial_value.astype(jnp.bfloat16), "factor", scatter_dimension=0, tiled=True
     )
-    shard_part = lax.all_gather(act_in, "dp", axis=0, tiled=True)
+    shard_part = swapped_in(act_in, "dp", 0)
     flattened = shard_part.reshape(-1, shard_part.shape[2])
     product = jnp.dot(flattened, basis_in, preferred_element_type=jnp.float32)
     act_part = product.reshape(shard_part.shape[0], shard_part.shape[1], -1)

time: 581 us -> 466 us (0.80); the launches traced: 581 us -> 458 us
  waiting for transfers between devices: 414 us -> 182 us
  blocking collectives: 104 us -> 212 us
    all_to_all x0 -> x1, blocking collectives: none -> 106 us  [swapped_in(): return jnp.concatenate(lax.all_to_all(outgoing, axis, 0, 0), axis=d)]
    all_gather x1 -> x0, waiting for transfers between devices: 65.9 us -> none  [shards(): shard_part = lax.all_gather(act_in, 'dp', axis=0, tiled=True)]
    all_gather x1, waiting for transfers between devices: 55.1 us -> 0.03 us  [shards(): lax.all_gather(value_sum.astype(jnp.bfloat16), 'dp', axis=2, tiled=True)]
    reduce_scatter x1, waiting for transfers between devices: 50.1 us -> 1.48 us  [shards(): lax.psum_scatter(partial_value.astype(jnp.bfloat16), 'factor', scatter_di...]
    all_gather x1, waiting for transfers between devices: 102 us -> 53.7 us  [shards(): shard_part = lax.all_gather(grad_out, 'dp', axis=0, tiled=True)]
    psum x1, waiting for transfers between devices: 71.2 us -> 49.5 us  [shards(): lax.psum(query_part.astype(jnp.bfloat16), 'factor').astype(jnp.float32)]
    reduce_scatter x1, waiting for transfers between devices: 5.17 us -> 12.1 us  [shards(): lax.psum_scatter(act_part.astype(jnp.bfloat16), 'factor', scatter_dimensi...]
  transfers between devices with their start and end apart: 7 -> 6, of which waited for: 7 -> 5; matrix products, arithmetic and copies ran while one was open for 3% -> 4% of each run, Pallas kernels for 0% -> 0%
where the time goes in v1:
time: 466 us; the launch traced here: 458 us
  blocking collectives  212 us (45%)
  waiting for transfers between devices  182 us (39%)
  matrix products  39.2 us (8%)
  between operations  14.9 us (3%)
  other arithmetic  6.81 us (1%)
    all_to_all x1, blocking collectives, swapped_in(): return jnp.concatenate(lax.all_to_all(outgoing, axis, 0, 0), axis=d)  106 us
    psum x1, blocking collectives, shards(): return lax.psum(partial_scores, 'dp')  72.7 us
    all_gather x1, waiting for transfers between devices, shards(): act_rot = lax.all_gather(act_sum, 'dp', axis=2, tiled=True)  64.8 us
    all_gather x1, waiting for transfers between devices, shards(): shard_part = lax.all_gather(grad_out, 'dp', axis=0, tiled=True)  53.7 us
    psum x1, waiting for transfers between devices, shards(): lax.psum(query_part.astype(jnp.bfloat16), 'factor').astype(jnp.float32)  49.5 us
    psum x1, blocking collectives, shards(): lax.psum(value_part.astype(jnp.bfloat16), 'factor').astype(jnp.float32)  34.2 us
    dot_general x4, matrix products, per_sequence(): lax.dot_general(scaled, value_mat, (((1,), (1,)), ((), ())), preferred_el...  23.9 us
    reduce_scatter x1, waiting for transfers between devices, shards(): lax.psum_scatter(act_part.astype(jnp.bfloat16), 'factor', scatter_dimensi...  12.1 us
  transfers between devices with their start and end apart: 6, of which 5 were waited for; matrix products, arithmetic and copies ran while one was open for 4% of the time, Pallas kernels for 0%

profile of v1, /device:TPU:2, one launch (start us, length us, event | category | flops | bytes accessed | tf_op | source)
XLA Modules:
  0.0 457.5 jit_solution(14056458425171123841)
XLA Ops:
  7.4 0.0 copy-start
  7.4 0.0 reduce-scatter.5.cloned.1.call-start
  7.4 1.5 stack.2
  8.9 0.0 copy-start.1
  8.9 105.5 %all_to_all.5 = bf16[32,1,128,512]{3,2,1,0:T(8,128)(2,1)S(1)} all-to-all(bf16[32,1,128,512]{3,2,1,0:T(8,128)(2,1)S(1)} %stack.2), channel_id=1, replica_groups=mesh['dp'=32,'factor'=8] {'dp'}, dimensions={0} | all-to-all | bytes 8388608 | tf_op jit(solution)/shard_map/all_to_all | solution.py:9
  114.4 0.0 copy-done.1
  114.4 0.0 copy-start.2
  114.4 0.0 copy-start.3
  114.4 2.3 fusion.19
  116.7 0.0 reduce-scatter.5.cloned.1.call-update
  116.7 0.0 all-gather.4.cloned.1.call-start
  116.8 0.5 all-gather.4.cloned.1.call-update
  117.3 0.0 all-reduce.2.cloned.1.call-start
  117.3 0.0 copy-done
  117.4 0.0 copy-done.2
  117.4 1.3 fusion.22
  118.6 0.0 all-reduce.2.cloned.1.call-update
  118.6 0.0 all-gather.8.cloned.1.call-start
  118.7 0.0 copy-done.3
  118.7 0.2 convolution_convert_fusion.1
  118.9 34.2 %psum.21 = bf16[16,8,128]{2,1,0:T(8,128)(2,1)} all-reduce(bf16[16,8,128]{2,1,0:T(8,128)(2,1)S(1)} %convolution_convert_fusion.1), channel_id=1, replica_groups=mesh['dp'=32,'factor'=8] {'factor'}, use_global_device_ids=true, to_apply=%region_2.0 | all-reduce | flops 16384 | bytes 65536 | tf_op jit(solution)/shard_map/psum | solution.py:32
  153.1 0.0 all-gather.8.cloned.1.call-update
  153.1 0.0 all-gather.6.cloned.1.call-start
  153.2 12.1 %reduce-scatter.5.cloned.1.call-done = bf16[4,128,128]{2,1,0:T(8,128)(2,1)} async-done(((bf16[32,128,128]{2,1,0:T(8,128)(2,1)}), bf16[4,128,128]{2,1,0:T(8,128)(2,1)}) %reduce-scatter.5.cloned.1.call-update) | async-done | bytes 131088 | tf_op jit(solution)/shard_map/reduce_scatter | solution.py:24
  165.3 0.0 all-gather.6.cloned.1.call-update
  165.3 0.0 reduce-scatter.3.cloned.1.call-start
  165.4 53.7 %all-gather.4.cloned.1.call-done = bf16[32,128,1792]{2,1,0:T(8,128)(2,1)} async-done(((bf16[1,128,1792]{2,1,0:T(8,128)(2,1)}), bf16[32,128,1792]{2,1,0:T(8,128)(2,1)}) %all-gather.4.cloned.1.call-update) | async-done | bytes 14680080 | tf_op jit(solution)/shard_map/all_gather | solution.py:13
  219.1 11.6 %convolution_convert_fusion = bf16[32,128,448]{1,2,0:T(8,128)(2,1)} fusion(bf16[32,128,1792]{2,1,0:T(8,128)(2,1)} %all-gather.4.cloned.1.call-done, bf16[1792,448]{0,1:T(8,128)(2,1)S(1)} %copy-done), kind=kOutput, calls=%fused_computation.12 | convolution fusion | flops 6578503680 | bytes 19955712 | tf_op jit(solution)/shard_map/dot_general | solution.py:15
  230.7 0.0 reduce-scatter.3.cloned.1.call-update
  230.7 5.9 %convert_element_type.25 = f32[448,4096]{1,0:T(8,128)} convert(bf16[448,4096]{1,0:T(8,128)(2,1)} %param.13) | non-fusion elementwise | flops 1835008 | bytes 11010048 | tf_op jit(solution)/shard_map/convert_element_type | solution.py:38
  236.6 49.5 %all-reduce.2.cloned.1.call-done = bf16[16,8,448]{2,1,0:T(8,128)(2,1)} async-done(((bf16[16,8,448]{2,1,0:T(8,128)(2,1)}), bf16[16,8,448]{2,1,0:T(8,128)(2,1)}) %all-reduce.2.cloned.1.call-update) | async-done | bytes 114704 | tf_op jit(solution)/shard_map/psum | solution.py:31
  286.2 0.9 convert_element_type.28
  287.1 0.0 all-gather.8.cloned.1.call-done
  287.1 64.8 %all-gather.6.cloned.1.call-done = bf16[4,128,4096]{2,1,0:T(8,128)(2,1)} async-done(((bf16[4,128,128]{2,1,0:T(8,128)(2,1)}), bf16[4,128,4096]{2,1,0:T(8,128)(2,1)}) %all-gather.6.cloned.1.call-update) | async-done | bytes 4194320 | tf_op jit(solution)/shard_map/all_gather | solution.py:27
  351.9 1.5 reduce-scatter.3.cloned.1.call-done
  353.4 24.1 %while.10 = (s32[]{:T(128)}, f32[4,16]{1,0:T(4,128)S(1)}, bf16[4,128,448]{1,2,0:T(8,128)(2,1)}, bf16[4,128,4096]{2,1,0:T(8,128)(2,1)}, f32[448,4096]{1,0:T(8,128...) while((s32[]{:T(128)}, f32[4,16]{1,0:T(4,128)S(1)}, ...), condition=%wide.region_5.6_spmd, body=%wide.region_4.5_spmd.sunk | while | flops 943308800 | bytes 9782569 | solution.py:51
  353.4 6.0 %fusion.38 = f32[16]{0:T(128)S(1)} fusion(bf16[128,4096]{1,0:T(8,128)(2,1)} %get-tuple-element.144, f32[448,4096]{1,0:T(8,128)} %get-tuple-element.143, bf16[4,128,4096]{2,1,0:T(8,128)(2,1)} %get-tuple-element.142, s32[]{:T(128)S(6)} %copy.25, f32[16,8,448]{2,1,0:T(8,128)S(1)} %get-tuple-element.145, bf16[4,128,448]{1,2,0:T(8,128)(2,1)} %get-tuple-element.141), kind=kOutput, calls=%fused_computation.4.clone.1 | convolution fusion | flops 943308800 | bytes 9782336 | tf_op jit(solution)/shard_map/while/body/eval_jaxpr/dot_general | solution.py:45
  359.4 6.0 %fusion.38 = f32[16]{0:T(128)S(1)} fusion(bf16[128,4096]{1,0:T(8,128)(2,1)} %get-tuple-element.144, f32[448,4096]{1,0:T(8,128)} %get-tuple-element.143, bf16[4,128,4096]{2,1,0:T(8,128)(2,1)} %get-tuple-element.142, s32[]{:T(128)S(6)} %copy.25, f32[16,8,448]{2,1,0:T(8,128)S(1)} %get-tuple-element.145, bf16[4,128,448]{1,2,0:T(8,128)(2,1)} %get-tuple-element.141), kind=kOutput, calls=%fused_computation.4.clone.1 | convolution fusion | flops 943308800 | bytes 9782336 | tf_op jit(solution)/shard_map/while/body/eval_jaxpr/dot_general | solution.py:45
  365.4 6.0 %fusion.38 = f32[16]{0:T(128)S(1)} fusion(bf16[128,4096]{1,0:T(8,128)(2,1)} %get-tuple-element.144, f32[448,4096]{1,0:T(8,128)} %get-tuple-element.143, bf16[4,128,4096]{2,1,0:T(8,128)(2,1)} %get-tuple-element.142, s32[]{:T(128)S(6)} %copy.25, f32[16,8,448]{2,1,0:T(8,128)S(1)} %get-tuple-element.145, bf16[4,128,448]{1,2,0:T(8,128)(2,1)} %get-tuple-element.141), kind=kOutput, calls=%fused_computation.4.clone.1 | convolution fusion | flops 943308800 | bytes 9782336 | tf_op jit(solution)/shard_map/while/body/eval_jaxpr/dot_general | solution.py:45
  371.5 6.0 %fusion.38 = f32[16]{0:T(128)S(1)} fusion(bf16[128,4096]{1,0:T(8,128)(2,1)} %get-tuple-element.144, f32[448,4096]{1,0:T(8,128)} %get-tuple-element.143, bf16[4,128,4096]{2,1,0:T(8,128)(2,1)} %get-tuple-element.142, s32[]{:T(128)S(6)} %copy.25, f32[16,8,448]{2,1,0:T(8,128)S(1)} %get-tuple-element.145, bf16[4,128,448]{1,2,0:T(8,128)(2,1)} %get-tuple-element.141), kind=kOutput, calls=%fused_computation.4.clone.1 | convolution fusion | flops 943308800 | bytes 9782336 | tf_op jit(solution)/shard_map/while/body/eval_jaxpr/dot_general | solution.py:45
  377.5 72.7 %psum.23 = f32[4,16]{1,0:T(4,128)} all-reduce(f32[4,16]{1,0:T(4,128)S(1)} %get-tuple-element.42), channel_id=1, replica_groups=mesh['dp'=32,'factor'=8] {'dp'}, use_global_device_ids=true, to_apply=%region_6.7 | all-reduce | flops 64 | bytes 512 | tf_op jit(solution)/shard_map/psum | solution.py:52
  (5 shorter events, 0.1 us)
Async XLA Ops:
  7.4 110.0 %copy-start = (bf16[1792,448]{0,1:T(8,128)(2,1)S(1)}, bf16[1792,448]{0,1:T(8,128)(2,1)}, u32[]{:S(2)}) copy-start(bf16[1792,448]{0,1:T(8,128)(2,1)} %param.11) | copy-start | bytes 4816900
  7.4 157.9 %reduce-scatter.5.cloned.1.call-start = ((), (), s32[]{:S(2)}) async-start(), calls=%async_computation.5 | async-start | bytes 1179648 | tf_op jit(solution)/shard_map/reduce_scatter | solution.py:24
  8.9 105.6 %copy-start.1 = (bf16[512,128]{1,0:T(8,128)(2,1)S(1)}, bf16[512,128]{1,0:T(8,128)(2,1)}, u32[]{:S(2)}) copy-start(bf16[512,128]{1,0:T(8,128)(2,1)} %param.12) | copy-start | bytes 393220
  114.4 2.9 copy-start.2
  114.4 4.3 copy-start.3
  116.7 102.4 %all-gather.4.cloned.1.call-start = ((), (), s32[]{:S(2)}) async-start(), calls=%async_computation.3 | async-start | bytes 15138816 | tf_op jit(solution)/shard_map/all_gather | solution.py:13
  117.3 168.9 %all-reduce.2.cloned.1.call-start = ((), (), s32[]{:S(2)}) async-start(), calls=%async_computation.8 | async-start | bytes 262144 | tf_op jit(solution)/shard_map/psum | solution.py:31
  118.6 168.5 %all-gather.8.cloned.1.call-start = ((), (), s32[]{:S(2)}) async-start(), calls=%async_computation.7 | async-start | bytes 1081344 | tf_op jit(solution)/shard_map/all_gather | solution.py:34
  153.1 198.8 %all-gather.6.cloned.1.call-start = ((), (), s32[]{:S(2)}) async-start(), calls=%async_computation.6 | async-start | bytes 4325376 | tf_op jit(solution)/shard_map/all_gather | solution.py:27
  165.3 188.1 %reduce-scatter.3.cloned.1.call-start = ((), (), s32[]{:S(2)}) async-start(), calls=%async_computation.4 | async-start | bytes 4128768 | tf_op jit(solution)/shard_map/reduce_scatter | solution.py:17
Sparse Core Ops, SparseCore 0:
  116.8 48.4 reduce-scatter.4
  167.9 118.2 all-reduce.1
  288.7 64.6 reduce-scatter.2
Sparse Core Ops, SparseCore 1:
  119.7 99.3 all-gather.3
  221.4 61.3 all-gather.7
  285.1 66.7 all-gather.5
